TPU v7x, 128 devices: a whole 4x4x4 slice. The times are simulated.
128 devices in a mesh: pool: 8 (over x, core), wide: 8 (over y, z_hi), narrow: 2 (over z_lo).
Axes of the slice: x: 4, y: 4, z: 4 (z_hi: 2, z_lo: 2; z = z_hi * 2 + z_lo), core: 2. Of those that a mesh axis runs over, the one named last changes fastest.
Arguments:
- states: bfloat16 [384, 2560], P('pool'), may hold values from -3 to 3
- gain_in: float32 [2560], replicated, may hold values from 0.1 to 1.9
- w_qkv: bfloat16 [2560, 8, 6, 128], P('narrow', 'wide'), may hold values from -0.125 to 0.125
- q_gain: float32 [128], replicated, may hold values from 0.1 to 1.9
- k_gain: float32 [128], replicated, may hold values from 0.1 to 1.9
- key_cache: bfloat16 [2304, 8, 128, 128], P('pool', 'wide', 'narrow'), as said below
- value_cache: bfloat16 [2304, 8, 128, 128], P('pool', 'wide', 'narrow'), may hold values from -12 to 12
- cache_len: int32 [384], replicated, may hold values from 1 to 8192, as said below
- page_table: int32 [384, 64], replicated, may hold values from -1 to 2303, as said below
- w_out: bfloat16 [4096, 2560], P('wide'), may hold values from -0.125 to 0.125
- gain_post: float32 [2560], replicated, may hold values from 0.1 to 1.9
- w_gate_up: bfloat16 [2560, 2, 9728], P(None, None, ('wide', 'narrow')), may hold values from -0.125 to 0.125
- w_down: bfloat16 [9728, 2560], P(('wide', 'narrow')), may hold values from -0.078125 to 0.078125
Outputs:
- attn_mixed: bfloat16 [384, 2560], P('pool')
- layer_out: bfloat16 [384, 2560], P('pool')
Inputs may be any that keep to these rules, and one draw needn't show every extreme that they name: `cache_len`: exactly one request has 8192 cached tokens; every other request has at most (5) * 128. `page_table`: entry (r, b) is pool device times 288 plus slot of the page with tokens b * 128 to (b + 1) * 128 - 1 of request r for b < ceil(cache_len[r] / 128), and -1 for later b; no slot is named twice. One pool device holds exactly 288 pages; the others hold the remaining pages, within one page of each other. `key_cache`: cached keys.
All inputs are finite; a program needn't handle non-finite values.
Results may differ from a plain program's by a relative error of at most 0.012.
The roundings to bfloat16 on the way count: a program that leaves them out, or rounds other values in their place, can miss the bound.
Values may be sent and summed in bfloat16 or wider, within the bound.
No kernel may reach another device: no remote copies, remote signals or barrier semaphores. Data moves between devices by JAX's collectives and lax.ppermute only.
A program may use at most 128 MiB of HBM per device.

v0:
```python
import math

import jax
import jax.numpy as jnp
from jax import lax
from jax.sharding import PartitionSpec as P

epsilon = 1e-06
rope_base = 1000000.0
masked_score = -1e30


def rms_scale(values, gain):
    return values * lax.rsqrt(jnp.mean(values * values, axis=-1, keepdims=True) + epsilon) * gain


def rotate(values, angle_pos):
    half = values.shape[-1] // 2
    ramp = jnp.arange(half).astype(jnp.float32)
    freqs = jnp.exp(ramp * (-2.0 * math.log(rope_base) / values.shape[-1]))
    angle = angle_pos[..., None] * freqs
    cosine = jnp.cos(angle)
    sine = jnp.sin(angle)
    lower = values[..., :half]
    upper = values[..., half:]
    return jnp.concatenate([lower * cosine - upper * sine, upper * cosine + lower * sine], axis=-1)


def feed_forward(normed_post, w_gate_up):
    gate_up = jnp.einsum("rd,dcf->rcf", normed_post, w_gate_up, preferred_element_type=jnp.float32)
    return (jax.nn.silu(gate_up[:, 0]) * gate_up[:, 1]).astype(jnp.bfloat16)


def per_device(
    states,
    gain_in,
    w_qkv,
    q_gain,
    k_gain,
    key_cache,
    value_cache,
    cache_len,
    page_table,
    w_out,
    gain_post,
    w_gate_up,
    w_down,
):
    kv_local = w_qkv.shape[1]
    group = w_qkv.shape[2] - 2
    head_dim = w_qkv.shape[3]
    scale = head_dim ** (-0.5)
    narrow_size = lax.axis_size("narrow")
    narrow_index = lax.axis_index("narrow")
    pool_index = lax.axis_index("pool")
    resid_in = states.astype(jnp.float32)
    normed = rms_scale(resid_in, gain_in).astype(jnp.bfloat16)
    part_width = w_qkv.shape[0]
    own_part = lax.dynamic_slice_in_dim(normed, narrow_index * part_width, part_width, 1)
    partial_proj = jnp.einsum("rd,dkch->rkch", own_part, w_qkv, preferred_element_type=jnp.float32)
    proj = lax.psum_scatter(partial_proj, "narrow", scatter_dimension=0, tiled=True)
    row_count = proj.shape[0]
    first_row = (pool_index * narrow_size + narrow_index) * row_count
    own_len = lax.dynamic_slice_in_dim(cache_len, first_row, row_count, 0)
    position = own_len.astype(jnp.float32)
    query = rotate(
        rms_scale(proj[:, :, :group], q_gain),
        jnp.broadcast_to(position[:, None, None], (row_count, kv_local, group)),
    ).astype(jnp.bfloat16)
    key_new = rotate(rms_scale(proj[:, :, group], k_gain), position[:, None]).astype(jnp.bfloat16)
    value_new = proj[:, :, group + 1].astype(jnp.bfloat16)
    all_queries = lax.all_gather(query, ("pool", "narrow"), axis=0, tiled=True)
    slot_count = key_cache.shape[0]
    half_page = key_cache.shape[2]
    holder_count = lax.axis_size("pool")
    req_count = page_table.shape[0]
    max_blocks = page_table.shape[1]
    flat_pages = page_table.reshape(-1)
    entry = jnp.arange(req_count * max_blocks, dtype=jnp.int32)
    target = jnp.where(flat_pages >= 0, flat_pages, holder_count * slot_count)
    owner_all = (
        jnp.full((holder_count * slot_count,), -1, jnp.int32)
        .at[target]
        .set(entry // max_blocks, mode="drop")
    )
    block_all = (
        jnp.zeros((holder_count * slot_count,), jnp.int32)
        .at[target]
        .set(entry % max_blocks, mode="drop")
    )
    owner = lax.dynamic_slice_in_dim(owner_all, pool_index * slot_count, slot_count, 0)
    block = lax.dynamic_slice_in_dim(block_all, pool_index * slot_count, slot_count, 0)
    safe_owner = jnp.maximum(owner, 0)
    page_len = half_page * narrow_size
    token_pos = (
        block[:, None] * page_len
        + narrow_index * half_page
        + jnp.arange(half_page, dtype=jnp.int32)[None, :]
    )
    live = (owner[:, None] >= 0) & (token_pos < cache_len[safe_owner][:, None])
    live_mask = live[:, None, None, :]
    slot_query = all_queries[safe_owner]
    scores = (
        jnp.einsum("skgd,sktd->skgt", slot_query, key_cache, preferred_element_type=jnp.float32)
        * scale
    )
    slot_top = jnp.max(jnp.where(live_mask, scores, masked_score), axis=-1)
    member = owner[:, None] == jnp.arange(req_count, dtype=jnp.int32)[None, :]
    req_top = jnp.max(jnp.where(member[:, :, None, None], slot_top[:, None], masked_score), axis=0)
    expo = jnp.where(live_mask, jnp.exp(scores - req_top[safe_owner][..., None]), 0.0)
    slot_total = jnp.sum(expo, axis=-1)
    slot_out = jnp.einsum(
        "skgt,sktd->skgd",
        expo.astype(jnp.bfloat16),
        value_cache,
        preferred_element_type=jnp.float32,
    )
    member_weight = member.astype(jnp.float32)
    req_out = jnp.einsum(
        "sr,sx->rx",
        member_weight,
        slot_out.reshape(slot_count, -1),
        precision=lax.Precision.HIGHEST,
    )
    req_out = req_out.reshape(req_count, kv_local, group, head_dim)
    req_total = jnp.einsum(
        "sr,sx->rx",
        member_weight,
        slot_total.reshape(slot_count, -1),
        precision=lax.Precision.HIGHEST,
    )
    req_total = req_total.reshape(req_count, kv_local, group)
    got_out, got_top, got_total = (
        lax.all_to_all(req_out[None], ("pool", "narrow"), split_axis=1, concat_axis=0, tiled=True),
        lax.all_to_all(req_top[None], ("pool", "narrow"), split_axis=1, concat_axis=0, tiled=True),
        lax.all_to_all(
            req_total[None], ("pool", "narrow"), split_axis=1, concat_axis=0, tiled=True
        ),
    )
    own_score = (
        jnp.einsum("rkgd,rkd->rkg", query, key_new, preferred_element_type=jnp.float32) * scale
    )
    top = jnp.maximum(jnp.max(got_top, axis=0), own_score)
    factor = jnp.exp(got_top - top[None])
    own_expo = jnp.exp(own_score - top)
    total = jnp.sum(got_total * factor, axis=0) + own_expo
    own_term = jnp.einsum(
        "rkg,rkd->rkgd",
        own_expo.astype(jnp.bfloat16),
        value_new,
        preferred_element_type=jnp.float32,
    )
    summed = jnp.sum(got_out * factor[..., None], axis=0) + own_term
    attn = (
        (summed / total[..., None])
        .astype(jnp.bfloat16)
        .reshape(row_count, kv_local * group * head_dim)
    )
    partial_out = jnp.dot(
        lax.all_gather(attn, "narrow", axis=0, tiled=True),
        w_out,
        preferred_element_type=jnp.float32,
    )
    mixed = lax.psum(partial_out, "wide")
    resid = resid_in + mixed
    attn_mixed = mixed.astype(jnp.bfloat16)
    normed_post = rms_scale(resid, gain_post).astype(jnp.bfloat16)
    hidden = feed_forward(normed_post, w_gate_up)
    down = jnp.dot(hidden, w_down, preferred_element_type=jnp.float32)
    layer_out = (resid + lax.psum(down, ("wide", "narrow"))).astype(jnp.bfloat16)
    return (attn_mixed, layer_out)


def solution(mesh):
    in_specs = (
        P("pool", None),
        P(),
        P("narrow", "wide", None, None),
        P(),
        P(),
        P("pool", "wide", "narrow", None),
        P("pool", "wide", "narrow", None),
        P(),
        P(),
        P("wide", None),
        P(),
        P(None, None, ("wide", "narrow")),
        P(("wide", "narrow"), None),
    )
    out_specs = (P("pool", None), P("pool", None))
    return jax.shard_map(
        per_device, mesh=mesh, in_specs=in_specs, out_specs=out_specs, check_vma=False
    )
```

profile of v0, /device:TPU:0, one launch (start us, length us, event | category | flops | bytes accessed | tf_op | source)
XLA Modules:
  0.0 489.5 jit_solution(1775987561983351854)
XLA Ops:
  7.2 1.2 multiply_reduce_fusion.1
  8.5 1.8 convert_element_type.67
  10.3 0.8 dynamic-slice
  11.0 2.9 fusion.9
  14.0 0.7 fusion.32
  14.6 0.1 copy.62
  14.8 0.2 reshape.539
  14.9 0.2 compare_select_fusion
  15.1 90.5 %scatter_custom_fusion.1 = s32[2304]{0:T(1024)S(1)} fusion(s32[24576]{0:T(1024)S(1)} %bitcast.105, s32[24576]{0:T(1024)} %fusion.32, s32[]{:T(128)} %constant.29.clone.1), kind=kCustom, calls=%fused_computation.110 | custom fusion | bytes 9728 | tf_op jit(solution)/shard_map/scatter | solution.py:89
  105.6 90.2 %scatter_custom_fusion = s32[2304]{0:T(1024)S(1)} fusion(s32[24576]{0:T(1024)S(1)} %bitcast.106, s32[24576]{0:T(1024)S(1)} %add_select_fusion, s32[]{:T(128)} %constant.28.clone.1), kind=kCustom, calls=%fused_computation.112 | custom fusion | bytes 9220 | tf_op jit(solution)/shard_map/scatter | solution.py:84
  195.8 0.1 broadcast_compare_fusion
  195.9 0.1 multiply_add_fusion
  196.0 2.4 gather_fusion
  198.4 0.2 fusion.36
  198.6 0.1 dynamic-slice_convert_fusion
  198.7 0.8 iota_compare_fusion
  199.5 0.8 multiply_reduce_fusion.4
  200.3 0.9 multiply_reduce_fusion.3
  201.2 0.8 multiply_multiply_fusion.1
  202.0 0.7 fusion.76
  202.8 0.9 multiply_multiply_fusion
  203.6 0.1 fusion.54
  203.8 0.1 pad_maximum_fusion
  203.9 32.0 %all_gather.6 = bf16[384,1,4,128]{3,0,2,1:T(8,128)(2,1)S(1)} all-gather(bf16[24,1,4,128]{3,0,2,1:T(8,128)(2,1)S(1)} %pad_maximum_fusion), channel_id=1, replica_groups=mesh['pool'=8,'wide'=8,'narrow'=2] {'pool','narrow'}, dimensions={0}, use_global_device_ids=true | all-gather | bytes 417792 | tf_op jit(solution)/shard_map/all_gather | solution.py:72
  235.9 0.3 copy.63
  236.2 2.4 gather_fusion.1
  238.6 5.8 %select_reduce_fusion.1 = (f32[288,4]{1,0:T(8,128)S(1)}, f32[288,4,64]{2,1,0:T(4,128)}) fusion(pred[288,64]{1,0:T(8,128)(4,1)S(1)} %fusion.36, bf16[288,4,128]{2,1,0:T(4,128)(2,1)} %gather_fusion.1, bf16[288,1,64,128]{3,2,1,0:T(8,128)(2,1)} %param.18), kind=kOutput, calls=%fused_computation.23 | convolution fusion | flops 19094400 | bytes 5331456 | tf_op jit(solution)/shard_map/skgd,sktd->skgt/dot_general | solution.py:104
  244.5 0.1 copy.64
  244.5 0.3 select_reduce_fusion
  244.8 0.1 copy.65
  245.0 0.8 copy.68
  245.8 3.5 all-to-all-start.1
  249.3 1.7 gather_fusion.2
  251.1 1.9 fusion.16
  253.0 4.8 fusion
  257.9 1.4 fusion.29
  259.4 0.1 pad_maximum_fusion.1
  259.5 0.8 fusion.58
  260.2 1.3 fusion.70
  261.5 5.6 %all-to-all-start.2 = ((f32[1,384,1,4]{3,2,0,1:T(1,128)}), f32[1,384,1,4]{3,2,0,1:T(1,128)S(1)}, u32[]{:S(2)}, u32[]{:S(2)}) async-start(f32[1,384,1,4]{3,2,0,1:T(1,128)} %bitcast.101), calls=%async_computation.3 | async-start | bytes 393216 | tf_op jit(solution)/shard_map/all_to_all | solution.py:136
  267.2 2.0 convolution_bitcast_fusion
  269.1 1.4 copy.67
  270.5 0.6 reduce_max.32
  271.2 3.5 all-to-all-done.2
  274.7 0.7 copy-done.3
  275.4 4.3 all-to-all-start
  279.7 0.8 multiply_maximum_fusion
  280.5 0.6 copy-done.10
  281.1 0.7 subtract_exponential_fusion
  281.8 1.7 copy.69
  283.5 1.0 multiply_reduce_fusion.2
  284.5 0.7 convert_convert_fusion
  285.2 0.1 copy.71
  285.4 8.9 %all-to-all-done = f32[1,384,1,4,128]{4,3,2,0,1:T(4,128)} async-done(((f32[1,384,1,4,128]{4,3,2,0,1:T(4,128)}), f32[1,384,1,4,128]{4,3,2,0,1:T(4,128)}, u32[]{:S(2)}, u32[]{:S(2)}) %all-to-all-start) | async-done | bytes 786464 | tf_op jit(solution)/shard_map/all_to_all | solution.py:134
  294.3 1.4 fusion.12
  295.7 0.8 copy_bitcast_fusion
  296.5 4.5 all_gather.7
  301.0 3.1 fusion.81
  304.2 85.7 %all-reduce.3.cloned.1.call-done = f32[48,2560]{1,0:T(8,128)} async-done(((f32[48,2560]{1,0:T(8,128)}), f32[48,2560]{1,0:T(8,128)}) %all-reduce.3.cloned.1.call-update) | async-done | bytes 491536 | tf_op jit(solution)/shard_map/psum | solution.py:164
  389.9 1.2 multiply_reduce_fusion
  391.1 4.9 fusion.23
  396.1 1.4 fusion.50
  397.5 83.2 %all-reduce.5.cloned.1.call-done = f32[48,2560]{1,0:T(8,128)} async-done(((f32[48,2560]{1,0:T(8,128)}), f32[48,2560]{1,0:T(8,128)}) %all-reduce.5.cloned.1.call-update) | async-done | bytes 491536 | tf_op jit(solution)/shard_map/psum | solution.py:170
  480.8 2.2 add_convert_fusion
  (54 shorter events, 0.5 us)
Async XLA Ops:
  7.2 388.9 %copy-start = (bf16[608,2560]{1,0:T(8,128)(2,1)S(1)}, bf16[608,2560]{1,0:T(8,128)(2,1)}, u32[]{:S(2)}) copy-start(bf16[608,2560]{1,0:T(8,128)(2,1)} %param.25) | copy-start | bytes 9338884
  7.2 7.4 %copy-start.11 = (s32[384,64]{0,1:T(8,128)S(1)}, s32[384,64]{0,1:T(8,128)}, u32[]{:S(2)}) copy-start(s32[384,64]{0,1:T(8,128)} %param.21) | copy-start | bytes 294916
  7.2 188.8 %copy-start.1 = (s32[384]{0:T(512)S(1)}, s32[384]{0:T(512)}, u32[]{:S(2)}) copy-start(s32[384]{0:T(512)} %param.20) | copy-start | bytes 4612
  7.2 192.3 %reduce-scatter.2.cloned.1.call-start = ((), (), s32[]{:S(2)}) async-start(), calls=%async_computation.4 | async-start | bytes 221184 | tf_op jit(solution)/shard_map/reduce_scatter | solution.py:61
  10.3 192.5 %copy-start.18 = (f32[128]{0:T(128)S(1)}, f32[128]{0:T(128)}, u32[]{:S(2)}) copy-start(f32[128]{0:T(128)} %param.16) | copy-start | bytes 1540
  195.9 40.0 %copy-start.12 = (s32[288]{0:T(512)}, s32[288]{0:T(512)S(1)}, u32[]{:S(2)}) copy-start(s32[288]{0:T(512)S(1)} %get-tuple-element.3) | copy-start | bytes 3460
  195.9 48.5 %copy-start.14 = (s32[1024]{0:T(1024)}, s32[1024]{0:T(1024)S(1)}, u32[]{:S(2)}) copy-start(s32[1024]{0:T(1024)S(1)} %pad_clamp_fusion) | copy-start | bytes 12292
  198.6 45.8 %copy-start.5 = (pred[288,64]{1,0:T(8,128)(4,1)}, pred[288,64]{1,0:T(8,128)(4,1)S(1)}, u32[]{:S(2)}) copy-start(pred[288,64]{1,0:T(8,128)(4,1)S(1)} %fusion.36) | copy-start | bytes 55300
  203.8 32.1 %copy-start.6 = (bf16[24,1,4,64]{3,0,2,1:T(8,128)(2,1)}, bf16[24,1,4,64]{3,0,2,1:T(8,128)(2,1)S(1)}, u32[]{:S(2)}) copy-start(bf16[24,1,4,64]{3,0,2,1:T(8,128)(2,1)S(1)} %get-tuple-element.6) | copy-start | bytes 36868
  203.8 32.1 %copy-start.8 = (bf16[24,1,4,64]{3,0,2,1:T(8,128)(2,1)}, bf16[24,1,4,64]{3,0,2,1:T(8,128)(2,1)S(1)}, u32[]{:S(2)}) copy-start(bf16[24,1,4,64]{3,0,2,1:T(8,128)(2,1)S(1)} %get-tuple-element.7) | copy-start | bytes 36868
  238.6 5.9 %copy-start.4 = (pred[288,384]{1,0:T(8,128)(4,1)S(1)}, pred[288,384]{1,0:T(8,128)(4,1)}, u32[]{:S(2)}) copy-start(pred[288,384]{1,0:T(8,128)(4,1)} %iota_compare_fusion) | copy-start | bytes 331780
  245.8 15.7 %all-to-all-start.1 = ((f32[1,384,1,4]{3,2,0,1:T(1,128)}), f32[1,384,1,4]{3,2,0,1:T(1,128)S(1)}, u32[]{:S(2)}, u32[]{:S(2)}) async-start(f32[1,384,1,4]{3,2,0,1:T(1,128)} %copy.68), calls=%async_computation.2 | async-start | bytes 393216 | tf_op jit(solution)/shard_map/all_to_all | solution.py:135
  252.9 4.9 %copy-start.13 = (s32[288]{0:T(512)S(1)}, s32[288]{0:T(512)}, u32[]{:S(2)}) copy-start(s32[288]{0:T(512)} %copy-done.12) | copy-start | bytes 3460
  253.0 6.3 %copy-start.15 = (bf16[24,64]{1,0:T(8,128)(2,1)S(1)}, bf16[24,64]{1,0:T(8,128)(2,1)}, u32[]{:S(2)}) copy-start(bf16[24,64]{1,0:T(8,128)(2,1)} %get-tuple-element.10) | copy-start | bytes 9220
  253.0 6.3 %copy-start.16 = (bf16[24,64]{1,0:T(8,128)(2,1)S(1)}, bf16[24,64]{1,0:T(8,128)(2,1)}, u32[]{:S(2)}) copy-start(bf16[24,64]{1,0:T(8,128)(2,1)} %get-tuple-element.11) | copy-start | bytes 9220
  253.0 6.4 %copy-start.7 = (bf16[24,1,4,64]{3,0,2,1:T(8,128)(2,1)S(1)}, bf16[24,1,4,64]{3,0,2,1:T(8,128)(2,1)}, u32[]{:S(2)}) copy-start(bf16[24,1,4,64]{3,0,2,1:T(8,128)(2,1)} %copy-done.6) | copy-start | bytes 36868
  253.0 6.4 %copy-start.9 = (bf16[24,1,4,64]{3,0,2,1:T(8,128)(2,1)S(1)}, bf16[24,1,4,64]{3,0,2,1:T(8,128)(2,1)}, u32[]{:S(2)}) copy-start(bf16[24,1,4,64]{3,0,2,1:T(8,128)(2,1)} %copy-done.8) | copy-start | bytes 36868
  261.5 13.2 %all-to-all-start.2 = ((f32[1,384,1,4]{3,2,0,1:T(1,128)}), f32[1,384,1,4]{3,2,0,1:T(1,128)S(1)}, u32[]{:S(2)}, u32[]{:S(2)}) async-start(f32[1,384,1,4]{3,2,0,1:T(1,128)} %bitcast.101), calls=%async_computation.3 | async-start | bytes 393216 | tf_op jit(solution)/shard_map/all_to_all | solution.py:136
  274.7 0.7 copy-start.3
  275.4 19.0 %all-to-all-start = ((f32[1,384,1,4,128]{4,3,2,0,1:T(4,128)}), f32[1,384,1,4,128]{4,3,2,0,1:T(4,128)}, u32[]{:S(2)}, u32[]{:S(2)}) async-start(f32[1,384,1,4,128]{4,3,2,0,1:T(4,128)} %copy.67), calls=%async_computation.1 | async-start | bytes 1572864 | tf_op jit(solution)/shard_map/all_to_all | solution.py:134
  279.6 110.3 %copy-start.2 = (bf16[48,2560]{1,0:T(8,128)(2,1)S(1)}, bf16[48,2560]{1,0:T(8,128)(2,1)}, u32[]{:S(2)}) copy-start(bf16[48,2560]{1,0:T(8,128)(2,1)} %param.13) | copy-start | bytes 737284
  279.7 110.3 %all-reduce.3.cloned.1.call-start = ((), (), s32[]{:S(2)}) async-start(), calls=%async_computation.5 | async-start | bytes 983040 | tf_op jit(solution)/shard_map/psum | solution.py:164
  280.5 0.6 copy-start.10
  284.5 106.7 %copy-start.17 = (f32[2560]{0:T(1024)S(1)}, f32[2560]{0:T(1024)}, u32[]{:S(2)}) copy-start(f32[2560]{0:T(1024)} %param.23) | copy-start | bytes 30724
  304.2 176.6 %all-reduce.5.cloned.1.call-start = ((), (), s32[]{:S(2)}) async-start(), calls=%async_computation.6 | async-start | bytes 983040 | tf_op jit(solution)/shard_map/psum | solution.py:170
Sparse Core Ops, SparseCore 0:
  14.1 15.5 reduce-scatter.1
  304.3 85.5 all-reduce.2
  397.6 83.0 all-reduce.4
where the time goes:
time: 491 us; the launch traced here: 489 us
  local copies, waits for them, and re-layouts  194 us (40%)
  waiting for transfers between devices  181 us (37%)
  blocking collectives  36.5 us (7%)
  matrix products  27.1 us (6%)
  other arithmetic  22.4 us (5%)
  between operations  14.1 us (3%)
  starting transfers between devices  13.6 us (3%)
    scatter x1, local copies, waits for them, and re-layouts, per_device(): block_all = jnp.zeros((holder_count * slot_count,), jnp.int32).at[target]...  90.5 us
    scatter x1, local copies, waits for them, and re-layouts, per_device(): owner_all = jnp.full((holder_count * slot_count,), -1, jnp.int32).at[targ...  90.2 us
    psum x1, waiting for transfers between devices, per_device(): mixed = lax.psum(partial_out, 'wide')  85.7 us
    psum x1, waiting for transfers between devices, per_device(): lax.psum(down, ('wide', 'narrow'))  83.2 us
    all_gather x1, blocking collectives, per_device(): all_queries = lax.all_gather(query, ('pool', 'narrow'), axis=0, tiled=True)  32 us
  transfers between devices with their start and end apart: 6, of which 4 were waited for; matrix products, arithmetic and copies ran while one was open for 42% of the time, Pallas kernels for 0%

commit v1 on v0

v1 whole, which is shorter than its diff:
```python
import functools
import math

import jax
import jax.numpy as jnp
from jax import lax
from jax.experimental import pallas as pl
from jax.experimental.pallas import tpu as pltpu
from jax.sharding import PartitionSpec as P

epsilon = 1e-06
rope_base = 1000000.0
masked_score = -1e30
lane = 128
unit_pad = 64
short_pages = 5
code_span = 128
f32 = jnp.float32
bf16 = jnp.bfloat16


def call(kernel, out_shapes, operands, scratch=(), scalars=0, limit=24):
    smem = pl.BlockSpec(memory_space=pltpu.SMEM)
    vmem = pl.BlockSpec(memory_space=pltpu.VMEM)
    single = isinstance(out_shapes, tuple)
    outs = [out_shapes] if single else out_shapes
    result = pl.pallas_call(
        kernel,
        out_shape=[jax.ShapeDtypeStruct(*o) for o in outs],
        in_specs=[smem] * scalars + [vmem] * (len(operands) - scalars),
        out_specs=[vmem] * len(outs),
        scratch_shapes=list(scratch),
        compiler_params=pltpu.CompilerParams(vmem_limit_bytes=limit << 20),
    )(*operands)
    return result[0] if single else result


def exchange(blocks, axes):
    return lax.all_to_all(blocks, axes, split_axis=0, concat_axis=0, tiled=True)


def project_kernel(n_ref, states_ref, gain_ref, w_ref, out_ref, normed_ref):
    parts, part_width, head_dim = w_ref.shape
    x = states_ref[...].astype(f32)
    inverse = lax.rsqrt(jnp.mean(x * x, axis=-1, keepdims=True) + epsilon)
    normed_ref[...] = (x * inverse * gain_ref[...]).astype(bf16)
    start = pl.multiple_of(n_ref[0] * part_width, lane)
    own = normed_ref[:, pl.ds(start, part_width)]
    for c in range(parts):
        out_ref[:, c * head_dim : (c + 1) * head_dim] = jnp.dot(
            own, w_ref[c], preferred_element_type=f32
        )


def query_kernel(own_ref, other_ref, cos_ref, sin_ref, qg_ref, kg_ref, rows_ref, send_ref):
    head_dim = cos_ref.shape[1]
    copies, _, width = send_ref.shape
    group = width // head_dim
    proj = own_ref[...] + other_ref[...]
    cosine, sine = cos_ref[...], sin_ref[...]
    for c in range(group + 1):
        u = proj[:, c * head_dim : (c + 1) * head_dim]
        gain = qg_ref[...] if c < group else kg_ref[...]
        u = u * lax.rsqrt(jnp.mean(u * u, axis=-1, keepdims=True) + epsilon) * gain
        v = (u * cosine + pltpu.roll(u, head_dim // 2, 1) * sine).astype(bf16)
        rows_ref[:, c * head_dim : (c + 1) * head_dim] = v.astype(f32)
        if c < group:
            for d in range(copies):
                send_ref[d, :, c * head_dim : (c + 1) * head_dim] = v
    c = group + 1
    rows_ref[:, c * head_dim : (c + 1) * head_dim] = (
        proj[:, c * head_dim : (c + 1) * head_dim].astype(bf16).astype(f32)
    )


def slot_kernel(p_ref, n_ref, pages_ref, len_ref, member_ref, count_ref, owner_ref):
    slot_count, req_count = member_ref.shape
    max_blocks = pages_ref.shape[0]
    half_page = code_span // 2
    first_slot = (p_ref[0] * slot_count).astype(f32)
    first_token = (n_ref[0] * half_page).astype(f32)
    lengths = len_ref[...].astype(f32)
    pages = pages_ref[...].astype(f32)
    request = lax.broadcasted_iota(jnp.int32, (1, req_count), 1).astype(f32)
    slot = lax.broadcasted_iota(jnp.int32, (slot_count, 1), 0).astype(f32) + first_slot
    code = jnp.full((slot_count, req_count), -1.0, f32)
    for b in range(short_pages):
        live = jnp.clip(lengths - (b * code_span) - first_token, 0.0, float(half_page))
        code = jnp.where(pages[b : b + 1] == slot, request * code_span + live, code)
    code = jnp.max(code, axis=1, keepdims=True)
    length = jnp.max(lengths, axis=1, keepdims=True)
    longest = lengths == length
    number = jnp.sum(jnp.where(longest, request, 0.0), axis=1, keepdims=True)
    column = jnp.sum(jnp.where(longest, pages, 0.0), axis=1, keepdims=True)
    column = jnp.concatenate(
        [column, jnp.full((lane - max_blocks, 1), -1.0, f32)], axis=0
    )
    row = jnp.transpose(jnp.broadcast_to(column, (lane, lane)))[:1]
    block = lax.broadcasted_iota(jnp.int32, (1, lane), 1).astype(f32)
    live = jnp.clip(length - block * code_span - first_token, 0.0, float(half_page))
    found = jnp.where(row == slot, number * code_span + live, -1.0)
    code = jnp.maximum(code, jnp.max(found, axis=1, keepdims=True))
    owner = jnp.floor(code * (1.0 / code_span))
    count_ref[...] = jnp.broadcast_to(
        jnp.where(code >= 0, code - owner * code_span, 0.0), count_ref.shape
    )
    member_ref[...] = jnp.where(owner == request, 1.0, 0.0).astype(bf16)
    padded = owner_ref.shape[1]
    wide = jnp.broadcast_to(owner, (slot_count, lane))
    wide = jnp.concatenate([wide, jnp.full((padded - slot_count, lane), -1.0, f32)], axis=0)
    owner_ref[...] = jnp.transpose(wide)[: owner_ref.shape[0]]


def attend_kernel(
    q_ref,
    k_ref,
    v_ref,
    member_ref,
    count_ref,
    owner_ref,
    out_ref,
    qs_ref,
    o_ref,
    ml_ref,
    req_ref,
):
    slot_count, half_page, head_dim = k_ref.shape
    req_count = member_ref.shape[1]
    padded = ml_ref.shape[0]
    group = o_ref.shape[0]
    peers = out_ref.shape[0]
    rows = req_count // peers
    scale = head_dim ** (-0.5)
    block = 8
    queries = q_ref[...].reshape(req_count, group * head_dim)
    qs_ref[...] = jnp.dot(member_ref[...], queries, preferred_element_type=f32)
    columns = block * half_page
    relative = lax.broadcasted_iota(jnp.int32, (block, columns), 1) - (
        half_page * lax.broadcasted_iota(jnp.int32, (block, columns), 0)
    )
    relative = relative.astype(f32)
    positive = relative >= 0.0
    spot = lax.broadcasted_iota(jnp.int32, (block, lane), 1)
    o_ref[:, slot_count:, :] = jnp.zeros((group, padded - slot_count, head_dim), bf16)
    ml_ref[slot_count:, :] = jnp.where(
        lax.broadcasted_iota(jnp.int32, (padded - slot_count, lane), 1) < group, masked_score, 0.0
    )

    def step(i, carry):
        outs = []
        for half in range(2):
            base = pl.multiple_of(i * (2 * block) + half * block, block)
            qb = qs_ref[pl.ds(base, block), :]
            q = jnp.concatenate(
                [qb[:, g * head_dim : (g + 1) * head_dim] for g in range(group)], axis=0
            ).astype(bf16)
            k = k_ref[pl.ds(base, block)].reshape(columns, head_dim)
            v = v_ref[pl.ds(base, block)].reshape(columns, head_dim)
            s = lax.dot_general(q, k, (((1,), (1,)), ((), ())), preferred_element_type=f32)
            s = s.reshape(group, block, columns) * scale
            count = count_ref[pl.ds(base, block), :1]
            live = (positive & (relative < count))[None]
            s = jnp.where(live, s, masked_score)
            top = jnp.max(s, axis=-1, keepdims=True)
            p = jnp.where(live, jnp.exp(s - top), 0.0)
            total = jnp.sum(p, axis=-1, keepdims=True)
            o = jnp.dot(
                p.reshape(group * block, columns).astype(bf16), v, preferred_element_type=f32
            )
            outs.append(o.reshape(group, block, head_dim))
            stat = jnp.zeros((block, lane), f32)
            for g in range(group):
                stat = jnp.where(spot == g, top[g], stat)
                stat = jnp.where(spot == group + g, total[g], stat)
            ml_ref[pl.ds(base, block), :] = stat
        base = pl.multiple_of(i * (2 * block), 2 * block)
        o_ref[:, pl.ds(base, 2 * block), :] = jnp.concatenate(outs, axis=1).astype(bf16)
        return carry

    lax.fori_loop(0, slot_count // (2 * block), step, 0, unroll=2)

    stats = jnp.transpose(ml_ref[...])
    request = lax.broadcasted_iota(jnp.int32, (req_count, 1), 0).astype(f32)
    member = request == owner_ref[:1, :]
    spot = lax.broadcasted_iota(jnp.int32, (req_count, lane), 1)
    summary = jnp.zeros((req_count, lane), f32)
    for g in range(group):
        tops = jnp.where(member, stats[g : g + 1], masked_score)
        top = jnp.max(tops, axis=1, keepdims=True)
        weight = jnp.where(member, jnp.exp(tops - top), 0.0)
        total = jnp.sum(weight * stats[group + g : group + g + 1], axis=1, keepdims=True)
        req_ref[g] = jnp.dot(weight.astype(bf16), o_ref[g], preferred_element_type=f32)
        summary = jnp.where(spot == g, top, summary)
        summary = jnp.where(spot == group + g, total, summary)
    high = summary.astype(bf16).astype(f32)
    left = summary - high
    middle = left.astype(bf16).astype(f32)
    low = (left - middle).astype(bf16).astype(f32)
    req_ref[group] = (
        high + pltpu.roll(middle, 2 * group, 1) + pltpu.roll(low, 4 * group, 1)
    )
    blank = jnp.zeros((out_ref.shape[1] - (group + 1) * rows, lane), f32)
    for d in range(peers):
        pieces = [req_ref[g, d * rows : (d + 1) * rows, :] for g in range(group + 1)]
        out_ref[d] = jnp.concatenate(pieces + [blank], axis=0).astype(bf16)


def write_units(units_ref, values, out_ref, first, step, parts, units):
    rows, width = values.shape
    for c in range(width // lane):
        units_ref[c * rows : (c + 1) * rows, :] = values[:, c * lane : (c + 1) * lane]
    for w in range(parts):
        out_ref[first + step * w] = units_ref[w * units : w * units + unit_pad, :].astype(bf16)


def combine_kernel(n_ref, got_ref, rows_ref, w_ref, out_ref, units_ref):
    peers = got_ref.shape[0]
    group = w_ref.shape[0] // lane
    rows = rows_ref.shape[0] // 2
    parts = out_ref.shape[0]
    units = rows * w_ref.shape[1] // lane // parts
    scale = lane ** (-0.5)
    own = rows_ref[pl.ds(pl.multiple_of(n_ref[0] * rows, 8), rows), :]
    key = own[:, group * lane : (group + 1) * lane]
    value = own[:, (group + 1) * lane : (group + 2) * lane]
    spot = lax.broadcasted_iota(jnp.int32, (rows, lane), 1)
    own_score = jnp.full((rows, lane), masked_score, f32)
    for g in range(group):
        score = jnp.sum(own[:, g * lane : (g + 1) * lane] * key, axis=1, keepdims=True) * scale
        own_score = jnp.where(spot == g, score, own_score)
    top = own_score
    stats = []
    for d in range(peers):
        packed = got_ref[d, group * rows : (group + 2) * rows, :].astype(f32)[:rows]
        stat = (
            packed
            + pltpu.roll(packed, lane - 2 * group, 1)
            + pltpu.roll(packed, lane - 4 * group, 1)
        )
        stats.append(stat)
        top = jnp.maximum(top, jnp.where(spot < group, stat, masked_score))
    own_expo = jnp.exp(own_score - top)
    total = own_expo
    sums = [
        own_expo[:, g : g + 1].astype(bf16).astype(f32) * value for g in range(group)
    ]
    for d in range(peers):
        factor = jnp.where(spot < group, jnp.exp(stats[d] - top), 0.0)
        total = total + factor * pltpu.roll(stats[d], lane - group, 1)
        got = got_ref[d].astype(f32)
        for g in range(group):
            sums[g] = sums[g] + factor[:, g : g + 1] * got[g * rows : (g + 1) * rows]
    attn = jnp.concatenate(
        [(sums[g] / total[:, g : g + 1]).astype(bf16) for g in range(group)], axis=1
    )
    mixed = jnp.dot(attn, w_ref[...], preferred_element_type=f32)
    units_ref[rows * mixed.shape[1] // lane :, :] = jnp.zeros((8, lane), f32)
    write_units(units_ref, mixed, out_ref, 0, 1, parts, units)


def residual_kernel(w_ref, n_ref, got_ref, states_ref, send_ref, resid_ref, units_ref):
    parts = got_ref.shape[0]
    rows = states_ref.shape[0] // 2
    width = states_ref.shape[1]
    units = rows * width // lane // parts
    mixed = got_ref[0].astype(f32)
    for w in range(1, parts):
        mixed = mixed + got_ref[w].astype(f32)
    for d in range(send_ref.shape[0]):
        send_ref[d] = mixed.astype(bf16)
    states = states_ref[...].astype(f32)
    states = jnp.where(n_ref[0] == 0, states[:rows], states[rows:])
    for c in range(width // lane):
        units_ref[c * rows : (c + 1) * rows, :] = states[:, c * lane : (c + 1) * lane]
    units_ref[rows * width // lane :, :] = jnp.zeros((8, lane), f32)
    for w in range(parts):

        @pl.when(w_ref[0] == w)
        def _():
            resid_ref[...] = mixed + units_ref[w * units : w * units + unit_pad, :]


def read_units(got_ref, units_ref, parts, units):
    for w in range(parts):
        for n in range(2):
            units_ref[n, w * units : (w + 1) * units, :] = got_ref[2 * w + n].astype(f32)[:units]


def hidden_kernel(
    got_ref, states_ref, gain_ref, wg_ref, wd_ref, mixed_ref, out_ref, units_ref, x_ref, flat_ref
):
    rows, width = states_ref.shape
    half = rows // 2
    parts = got_ref.shape[0] // 2
    units = half * width // lane // parts
    read_units(got_ref, units_ref, parts, units)
    square = jnp.zeros((rows, lane), f32)
    for c in range(width // lane):
        span = slice(c * lane, (c + 1) * lane)
        mixed = jnp.concatenate(
            [units_ref[n, c * half : (c + 1) * half, :] for n in range(2)], axis=0
        )
        mixed_ref[:, span] = mixed.astype(bf16)
        resid = states_ref[:, span].astype(f32) + mixed
        x_ref[:, span] = resid
        square = square + resid * resid
    inverse = lax.rsqrt(jnp.sum(square, axis=1, keepdims=True) * (1.0 / width) + epsilon)
    normed = (x_ref[...] * inverse * gain_ref[...]).astype(bf16)
    contract = (((1,), (1,)), ((), ()))
    gate = lax.dot_general(normed, wg_ref[0], contract, preferred_element_type=f32)
    up = lax.dot_general(normed, wg_ref[1], contract, preferred_element_type=f32)
    hidden = (gate / (1.0 + jnp.exp(-gate)) * up).astype(bf16)
    down = jnp.dot(hidden, wd_ref[...], preferred_element_type=f32)
    flat_ref[half * width // lane :, :] = jnp.zeros((8, lane), f32)
    for n in range(2):
        write_units(flat_ref, down[n * half : (n + 1) * half], out_ref, n, 2, parts, units)


def total_kernel(got_ref, resid_ref, send_ref):
    out = got_ref[0].astype(f32)
    for d in range(1, got_ref.shape[0]):
        out = out + got_ref[d].astype(f32)
    out = (resid_ref[...] + out).astype(bf16)
    for d in range(send_ref.shape[0]):
        send_ref[d] = out


def gather_kernel(got_ref, out_ref, units_ref):
    rows, width = out_ref.shape
    half = rows // 2
    parts = got_ref.shape[0] // 2
    units = half * width // lane // parts
    read_units(got_ref, units_ref, parts, units)
    for c in range(width // lane):
        block = jnp.concatenate(
            [units_ref[n, c * half : (c + 1) * half, :] for n in range(2)], axis=0
        )
        out_ref[:, c * lane : (c + 1) * lane] = block.astype(bf16)


def per_device(
    states,
    gain_in,
    w_qkv,
    q_gain,
    k_gain,
    key_cache,
    value_cache,
    cache_len,
    page_table,
    w_out,
    gain_post,
    w_gate_up,
    w_down,
):
    parts = w_qkv.shape[2]
    group = parts - 2
    head_dim = w_qkv.shape[3]
    narrow_size = lax.axis_size("narrow")
    wide_size = lax.axis_size("wide")
    holders = lax.axis_size("pool")
    peers = holders * narrow_size
    split = wide_size * narrow_size
    narrow = lax.axis_index("narrow").reshape(1)
    wide = lax.axis_index("wide").reshape(1)
    pool = lax.axis_index("pool").reshape(1)
    rows, width = states.shape
    half = rows // narrow_size
    req_count = page_table.shape[0]
    slot_count = key_cache.shape[0]
    half_page = key_cache.shape[2]
    keys = key_cache.reshape(slot_count, half_page, head_dim)
    values = value_cache.reshape(slot_count, half_page, head_dim)
    slot_pad = -(-slot_count // lane) * lane
    half_units = half * width // lane

    partial_proj = call(
        project_kernel,
        ((rows, parts * head_dim), f32),
        [narrow, states, gain_in[None], w_qkv[:, 0].swapaxes(0, 1)],
        [pltpu.VMEM((rows, width), bf16)],
        scalars=1,
    )
    swap = [(i, narrow_size - 1 - i) for i in range(narrow_size)]
    other_proj = lax.ppermute(partial_proj, "narrow", swap)
    own_len = lax.dynamic_slice_in_dim(cache_len, pool[0] * rows, rows, 0).astype(f32)
    ramp = jnp.arange(head_dim // 2).astype(f32)
    freqs = jnp.exp(ramp * (-2.0 * math.log(rope_base) / head_dim))
    angle = own_len[:, None] * freqs
    cosine, sine = jnp.cos(angle), jnp.sin(angle)
    cosine = jnp.concatenate([cosine, cosine], axis=1)
    sine = jnp.concatenate([-sine, sine], axis=1)
    member, count, owner = call(
        slot_kernel,
        [
            ((slot_count, req_count), bf16),
            ((slot_count, lane), f32),
            ((8, slot_pad), f32),
        ],
        [pool, narrow, page_table.T, cache_len[None]],
        scalars=2,
    )
    qkv_rows, sent = call(
        query_kernel,
        [((rows, parts * head_dim), f32), ((holders, rows, group * head_dim), bf16)],
        [partial_proj, other_proj, cosine, sine, q_gain[None], k_gain[None]],
    )
    queries = exchange(sent, "pool")
    payload = call(
        attend_kernel,
        ((peers, lane, lane), bf16),
        [queries, keys, values, member, count, owner],
        [
            pltpu.VMEM((slot_count, group * head_dim), f32),
            pltpu.VMEM((group, slot_pad, head_dim), bf16),
            pltpu.VMEM((slot_pad, lane), f32),
            pltpu.VMEM((group + 1, req_count, head_dim), f32),
        ],
    )
    got = exchange(payload, ("pool", "narrow"))
    sent = call(
        combine_kernel,
        ((wide_size, unit_pad, lane), bf16),
        [narrow, got, qkv_rows, w_out],
        [pltpu.VMEM((half_units + 8, lane), f32)],
        scalars=1,
    )
    got = exchange(sent, "wide")
    sent, resid_units = call(
        residual_kernel,
        [((split, unit_pad, lane), bf16), ((unit_pad, lane), f32)],
        [wide, narrow, got, states],
        [pltpu.VMEM((half_units + 8, lane), f32)],
        scalars=2,
    )
    both = ("wide", "narrow")
    got = exchange(sent, both)
    attn_mixed, sent = call(
        hidden_kernel,
        [((rows, width), bf16), ((split, unit_pad, lane), bf16)],
        [got, states, gain_post[None], w_gate_up.transpose(1, 2, 0), w_down],
        [
            pltpu.VMEM((narrow_size, half_units, lane), f32),
            pltpu.VMEM((rows, width), f32),
            pltpu.VMEM((half_units + 8, lane), f32),
        ],
    )
    got = exchange(sent, both)
    sent = call(total_kernel, ((split, unit_pad, lane), bf16), [got, resid_units])
    got = exchange(sent, both)
    layer_out = call(
        gather_kernel,
        ((rows, width), bf16),
        [got],
        [pltpu.VMEM((narrow_size, half_units, lane), f32)],
    )
    return (attn_mixed, layer_out)


def solution(mesh):
    in_specs = (
        P("pool", None),
        P(),
        P("narrow", "wide", None, None),
        P(),
        P(),
        P("pool", "wide", "narrow", None),
        P("pool", "wide", "narrow", None),
        P(),
        P(),
        P("wide", None),
        P(),
        P(None, None, ("wide", "narrow")),
        P(("wide", "narrow"), None),
    )
    out_specs = (P("pool", None), P("pool", None))
    return jax.shard_map(
        per_device, mesh=mesh, in_specs=in_specs, out_specs=out_specs, check_vma=False
    )
```

time: 491 us -> 119 us (0.24)
  local copies, waits for them, and re-layouts: 194 us -> 14.9 us
  waiting for transfers between devices: 181 us -> 26 us
  matrix products: 27.1 us -> 0 us
  other arithmetic: 22.4 us -> 1.02 us
  Pallas kernels: 0 us -> 19 us
  between operations: 14.1 us -> 0.76 us
    scatter x2 -> x0, local copies, waits for them, and re-layouts: 181 us -> none  [the longest x1 90.5 us: per_device(): block_all = jnp.zeros((holder_count * slot_count,), jnp.int32).at[target]...]
    psum x2 -> x0, waiting for transfers between devices: 169 us -> none  [the longest x1 85.7 us: per_device(): mixed = lax.psum(partial_out, 'wide')]
    all_to_all x0 -> x3, blocking collectives: none -> 38.9 us  [exchange(): return lax.all_to_all(blocks, axes, split_axis=0, concat_axis=0, tiled=True)]
    all_gather x2 -> x0, blocking collectives: 36.5 us -> none  [the longest x1 32 us: per_device(): all_queries = lax.all_gather(query, ('pool', 'narrow'), axis=0, tiled=True)]
    dot_general x9 -> x0, matrix products: 27.1 us -> none  [the longest x1 5.84 us: per_device(): jnp.einsum('skgd,sktd->skgt', slot_query, key_cache, preferred_element_ty...]
    pallas_call x0 -> x9, Pallas kernels: none -> 19 us  [call(): pl.pallas_call(kernel, out_shape=[jax.ShapeDtypeStruct(*o) for o in outs]...]
    unnamed x39 -> x28, local copies, waits for them, and re-layouts: 1.5 us -> 13.5 us
    all_to_all x3, waiting for transfers between devices: 12.5 us -> 23.1 us  [exchange(): return lax.all_to_all(blocks, axes, split_axis=0, concat_axis=0, tiled=True)]
  transfers between devices with their start and end apart: 6 -> 4, of which waited for: 4 -> 4; matrix products, arithmetic and copies ran while one was open for 42% -> 1% of each run, Pallas kernels for 0% -> 1%
where the time goes in v1:
time: 119 us
  blocking collectives  38.9 us (33%)
  waiting for transfers between devices  26 us (22%)
  Pallas kernels  19 us (16%)
  starting transfers between devices  18.1 us (15%)
  local copies, waits for them, and re-layouts  14.9 us (13%)
    all_to_all x3, blocking collectives, exchange(): return lax.all_to_all(blocks, axes, split_axis=0, concat_axis=0, tiled=True)  38.9 us
    all_to_all x3, waiting for transfers between devices, exchange(): return lax.all_to_all(blocks, axes, split_axis=0, concat_axis=0, tiled=True)  23.1 us
    pallas_call x9, Pallas kernels, call(): pl.pallas_call(kernel, out_shape=[jax.ShapeDtypeStruct(*o) for o in outs]...  19 us
    all_to_all x3, starting transfers between devices, exchange(): return lax.all_to_all(blocks, axes, split_axis=0, concat_axis=0, tiled=True)  16 us
    unnamed x28, local copies, waits for them, and re-layouts  13.5 us
    ppermute x1, waiting for transfers between devices, per_device(): other_proj = lax.ppermute(partial_proj, 'narrow', swap)  2.83 us
  transfers between devices with their start and end apart: 4, of which 4 were waited for; matrix products, arithmetic and copies ran while one was open for 1% of the time, Pallas kernels for 1%

profile of v1, /device:TPU:0, one launch (start us, length us, event | category | flops | bytes accessed | tf_op | source)
XLA Modules:
  0.0 118.6 jit_solution(1621051792934299383)
XLA Ops:
  0.6 0.7 broadcast_in_dim.17.gain_ref
  1.4 0.0 copy-start.5
  1.4 0.9 copy-done.5
  2.3 0.0 copy-start.7
  2.3 1.5 %copy-done.7 = bf16[1280,1,6,128]{3,0,2,1:T(8,128)(2,1)S(1)} copy-done((bf16[1280,1,6,128]{3,0,2,1:T(8,128)(2,1)S(1)}, bf16[1280,1,6,128]{3,0,2,1:T(8,128)(2,1)}, u32[]{:S(2)}) %copy-start.7) | copy-done | bytes 1966104
  3.8 0.5 shard_map.140.own_ref
  4.4 2.1 %collective-permute-start = (f32[48,768]{1,0:T(8,128)S(1)}, f32[48,768]{1,0:T(8,128)S(1)}, u32[]{:S(2)}, u32[]{:S(2)}) collective-permute-start(f32[48,768]{1,0:T(8,128)S(1)} %shard_map.140.own_ref), channel_id=1, source_target_pairs={{0,1},{1,0},{2,3},{3,2},{4,5},{5,4},{6,7},{7,6},{8,9},{9,8},{10,11... | collective-permute-start | bytes 442376 | tf_op jit(solution)/shard_map/ppermute | solution.py:385
  6.5 0.8 dynamic-slice_convert_fusion
  7.2 0.2 fusion
  7.4 0.1 pad_maximum_fusion
  7.5 2.8 %collective-permute-done.other_ref = f32[48,768]{1,0:T(8,128)S(1)} collective-permute-done((f32[48,768]{1,0:T(8,128)S(1)}, f32[48,768]{1,0:T(8,128)S(1)}, u32[]{:S(2)}, u32[]{:S(2)}) %collective-permute-start) | collective-permute-done | bytes 147488 | tf_op jit(solution)/shard_map/ppermute | solution.py:385
  10.3 0.0 copy-start.11
  10.3 0.7 copy-done.11
  11.0 0.0 copy-start.12
  11.0 0.7 copy-done.12
  11.6 1.0 shard_map.141
  12.6 4.3 %all-to-all-start = ((bf16[8,48,512]{2,1,0:T(8,128)(2,1)}), bf16[8,48,512]{2,1,0:T(8,128)(2,1)S(1)}, u32[]{:S(2)}, u32[]{:S(2)}) async-start(bf16[8,48,512]{2,1,0:T(8,128)(2,1)} %get-tuple-element.11), calls=%async_computation | async-start | bytes 786432 | tf_op jit(solution)/shard_map/all_to_all | solution.py:39
  16.9 0.7 broadcast_in_dim.20.len_ref
  17.6 0.0 copy-start.10
  17.6 0.9 copy-done.10
  18.5 0.6 shard_map.142
  19.1 6.8 %all-to-all-done.q_ref = bf16[8,48,512]{2,1,0:T(8,128)(2,1)S(1)} async-done(((bf16[8,48,512]{2,1,0:T(8,128)(2,1)}), bf16[8,48,512]{2,1,0:T(8,128)(2,1)S(1)}, u32[]{:S(2)}, u32[]{:S(2)}) %all-to-all-start) | async-done | bytes 393248 | tf_op jit(solution)/shard_map/all_to_all | solution.py:39
  25.9 0.0 copy-start.1
  25.9 2.3 %copy-done.1 = bf16[288,1,64,128]{3,2,1,0:T(8,128)(2,1)S(1)} copy-done((bf16[288,1,64,128]{3,2,1,0:T(8,128)(2,1)S(1)}, bf16[288,1,64,128]{3,2,1,0:T(8,128)(2,1)}, u32[]{:S(2)}) %copy-start.1) | copy-done | bytes 4718616
  28.2 0.0 copy-start.2
  28.2 2.3 %copy-done.2 = bf16[288,1,64,128]{3,2,1,0:T(8,128)(2,1)S(1)} copy-done((bf16[288,1,64,128]{3,2,1,0:T(8,128)(2,1)S(1)}, bf16[288,1,64,128]{3,2,1,0:T(8,128)(2,1)}, u32[]{:S(2)}) %copy-start.2) | copy-done | bytes 4718616
  30.5 0.0 copy-start.4
  30.5 11.5 %shard_map.143 = bf16[16,128,128]{2,1,0:T(8,128)(2,1)S(1)} custom-call(bf16[8,48,512]{2,1,0:T(8,128)(2,1)S(1)} %all-to-all-done.q_ref, bf16[288,64,128]{2,1,0:T(8,128)(2,1)S(1)} %bitcast.13, bf16[288,64,128]{2,1,0:T(8,128)(2,1)S(1)} %bitcast.14, bf16[288,384]{1,0:T(8,128)(2,1)S(1)} %get-tuple-element.12.member_ref, ...), custom_call_target="tpu_custom_call" | custom-call | tf_op jit(solution)/shard_map/pallas_call | solution.py:27
  42.1 0.0 copy-start.6
  42.1 0.0 copy-start.13
  42.1 0.0 copy-start.3
  42.1 15.0 %all_to_all.30.got_ref = bf16[16,128,128]{2,1,0:T(8,128)(2,1)S(1)} all-to-all(bf16[16,128,128]{2,1,0:T(8,128)(2,1)S(1)} %shard_map.143), channel_id=1, replica_groups=mesh['pool'=8,'wide'=8,'narrow'=2] {'pool','narrow'}, dimensions={0} | all-to-all | bytes 1048576 | tf_op jit(solution)/shard_map/all_to_all | solution.py:39
  57.2 0.0 copy-done.4
  57.2 1.0 shard_map.144
  58.2 0.0 copy-start.8
  58.2 0.7 copy-done.8
  58.9 7.5 %all-to-all-start.2 = ((bf16[8,64,128]{2,1,0:T(8,128)(2,1)}), bf16[8,64,128]{2,1,0:T(8,128)(2,1)S(1)}, u32[]{:S(2)}, u32[]{:S(2)}) async-start(bf16[8,64,128]{2,1,0:T(8,128)(2,1)} %copy-done.8), calls=%async_computation.2 | async-start | bytes 262144 | tf_op jit(solution)/shard_map/all_to_all | solution.py:39
  66.3 7.9 %all-to-all-done.2.got_ref = bf16[8,64,128]{2,1,0:T(8,128)(2,1)S(1)} async-done(((bf16[8,64,128]{2,1,0:T(8,128)(2,1)}), bf16[8,64,128]{2,1,0:T(8,128)(2,1)S(1)}, u32[]{:S(2)}, u32[]{:S(2)}) %all-to-all-start.2) | async-done | bytes 131104 | tf_op jit(solution)/shard_map/all_to_all | solution.py:39
  74.3 0.0 copy-done.6
  74.3 0.1 shard_map.145
  74.4 0.0 copy-start.9
  74.4 0.7 copy-done.9
  75.1 4.2 %all-to-all-start.3 = ((bf16[16,64,128]{2,1,0:T(8,128)(2,1)}), bf16[16,64,128]{2,1,0:T(8,128)(2,1)}, u32[]{:S(2)}, u32[]{:S(2)}) async-start(bf16[16,64,128]{2,1,0:T(8,128)(2,1)} %copy-done.9), calls=%async_computation.3 | async-start | bytes 524288 | tf_op jit(solution)/shard_map/all_to_all | solution.py:39
  79.3 0.0 copy-done.13
  79.3 8.5 %all-to-all-done.3.got_ref = bf16[16,64,128]{2,1,0:T(8,128)(2,1)} async-done(((bf16[16,64,128]{2,1,0:T(8,128)(2,1)}), bf16[16,64,128]{2,1,0:T(8,128)(2,1)}, u32[]{:S(2)}, u32[]{:S(2)}) %all-to-all-start.3) | async-done | bytes 262176 | tf_op jit(solution)/shard_map/all_to_all | solution.py:39
  87.8 0.0 copy-done.3
  87.8 0.0 copy-start
  87.8 2.8 %copy-done = bf16[2560,2,608]{0,2,1:T(8,128)(2,1)S(1)} copy-done((bf16[2560,2,608]{0,2,1:T(8,128)(2,1)S(1)}, bf16[2560,2,608]{0,2,1:T(8,128)(2,1)}, u32[]{:S(2)}) %copy-start) | copy-done | bytes 6225944
  90.5 3.4 %shard_map.146 = (bf16[48,2560]{1,0:T(8,128)(2,1)}, bf16[16,64,128]{2,1,0:T(8,128)(2,1)S(1)}) custom-call(bf16[16,64,128]{2,1,0:T(8,128)(2,1)} %all-to-all-done.3.got_ref, bf16[48,2560]{1,0:T(8,128)(2,1)S(1)} %copy-done.6, f32[1,2560]{1,0:T(1,128)S(1)} %broadcast_in_dim.21.gain_ref, bf16[2,608,2560]{2,1,0:T(8,128)(2,1)S(1)} %bitcast.12, ...), custom_call_target="tpu_custom_call" | custom-call | tf_op jit(solution)/shard_map/pallas_call | solution.py:27
  94.0 11.9 %all_to_all.31.got_ref = bf16[16,64,128]{2,1,0:T(8,128)(2,1)S(1)} all-to-all(bf16[16,64,128]{2,1,0:T(8,128)(2,1)S(1)} %get-tuple-element.18), channel_id=1, replica_groups=mesh['pool'=8,'wide'=8,'narrow'=2] {'wide','narrow'}, dimensions={0} | all-to-all | bytes 524288 | tf_op jit(solution)/shard_map/all_to_all | solution.py:39
  106.0 11.9 %all_to_all.32.got_ref = bf16[16,64,128]{2,1,0:T(8,128)(2,1)S(1)} all-to-all(bf16[16,64,128]{2,1,0:T(8,128)(2,1)S(1)} %shard_map.147), channel_id=1, replica_groups=mesh['pool'=8,'wide'=8,'narrow'=2] {'wide','narrow'}, dimensions={0} | all-to-all | bytes 524288 | tf_op jit(solution)/shard_map/all_to_all | solution.py:39
  117.9 0.7 shard_map.148
  (3 shorter events, 0.1 us)
Async XLA Ops:
  1.4 0.9 copy-start.5
  2.3 1.5 %copy-start.7 = (bf16[1280,1,6,128]{3,0,2,1:T(8,128)(2,1)S(1)}, bf16[1280,1,6,128]{3,0,2,1:T(8,128)(2,1)}, u32[]{:S(2)}) copy-start(bf16[1280,1,6,128]{3,0,2,1:T(8,128)(2,1)} %param.15) | copy-start | bytes 5898244
  4.4 5.9 %collective-permute-start = (f32[48,768]{1,0:T(8,128)S(1)}, f32[48,768]{1,0:T(8,128)S(1)}, u32[]{:S(2)}, u32[]{:S(2)}) collective-permute-start(f32[48,768]{1,0:T(8,128)S(1)} %shard_map.140.own_ref), channel_id=1, source_target_pairs={{0,1},{1,0},{2,3},{3,2},{4,5},{5,4},{6,7},{7,6},{8,9},{9,8},{10,11... | collective-permute-start | bytes 442376 | tf_op jit(solution)/shard_map/ppermute | solution.py:385
  10.3 0.7 copy-start.11
  11.0 0.7 copy-start.12
  12.6 13.2 %all-to-all-start = ((bf16[8,48,512]{2,1,0:T(8,128)(2,1)}), bf16[8,48,512]{2,1,0:T(8,128)(2,1)S(1)}, u32[]{:S(2)}, u32[]{:S(2)}) async-start(bf16[8,48,512]{2,1,0:T(8,128)(2,1)} %get-tuple-element.11), calls=%async_computation | async-start | bytes 786432 | tf_op jit(solution)/shard_map/all_to_all | solution.py:39
  17.6 0.9 copy-start.10
  25.9 2.3 %copy-start.1 = (bf16[288,1,64,128]{3,2,1,0:T(8,128)(2,1)S(1)}, bf16[288,1,64,128]{3,2,1,0:T(8,128)(2,1)}, u32[]{:S(2)}) copy-start(bf16[288,1,64,128]{3,2,1,0:T(8,128)(2,1)} %param.18) | copy-start | bytes 14155780
  28.2 2.3 %copy-start.2 = (bf16[288,1,64,128]{3,2,1,0:T(8,128)(2,1)S(1)}, bf16[288,1,64,128]{3,2,1,0:T(8,128)(2,1)}, u32[]{:S(2)}) copy-start(bf16[288,1,64,128]{3,2,1,0:T(8,128)(2,1)} %param.19) | copy-start | bytes 14155780
  30.5 26.6 %copy-start.4 = (bf16[512,2560]{1,0:T(8,128)(2,1)S(1)}, bf16[512,2560]{1,0:T(8,128)(2,1)}, u32[]{:S(2)}) copy-start(bf16[512,2560]{1,0:T(8,128)(2,1)} %w_ref.1) | copy-start | bytes 7864324
  42.1 32.2 %copy-start.6 = (bf16[48,2560]{1,0:T(8,128)(2,1)S(1)}, bf16[48,2560]{1,0:T(8,128)(2,1)}, u32[]{:S(2)}) copy-start(bf16[48,2560]{1,0:T(8,128)(2,1)} %states_ref.5) | copy-start | bytes 737284
  42.1 37.2 %copy-start.13 = (f32[2560]{0:T(1024)S(1)}, f32[2560]{0:T(1024)}, u32[]{:S(2)}) copy-start(f32[2560]{0:T(1024)} %param.23) | copy-start | bytes 30724
  42.1 45.6 %copy-start.3 = (bf16[608,2560]{1,0:T(8,128)(2,1)S(1)}, bf16[608,2560]{1,0:T(8,128)(2,1)}, u32[]{:S(2)}) copy-start(bf16[608,2560]{1,0:T(8,128)(2,1)} %wd_ref.1) | copy-start | bytes 9338884
  58.2 0.7 copy-start.8
  58.9 15.4 %all-to-all-start.2 = ((bf16[8,64,128]{2,1,0:T(8,128)(2,1)}), bf16[8,64,128]{2,1,0:T(8,128)(2,1)S(1)}, u32[]{:S(2)}, u32[]{:S(2)}) async-start(bf16[8,64,128]{2,1,0:T(8,128)(2,1)} %copy-done.8), calls=%async_computation.2 | async-start | bytes 262144 | tf_op jit(solution)/shard_map/all_to_all | solution.py:39
  74.4 0.7 copy-start.9
  75.1 12.7 %all-to-all-start.3 = ((bf16[16,64,128]{2,1,0:T(8,128)(2,1)}), bf16[16,64,128]{2,1,0:T(8,128)(2,1)}, u32[]{:S(2)}, u32[]{:S(2)}) async-start(bf16[16,64,128]{2,1,0:T(8,128)(2,1)} %copy-done.9), calls=%async_computation.3 | async-start | bytes 524288 | tf_op jit(solution)/shard_map/all_to_all | solution.py:39
  87.8 2.8 %copy-start = (bf16[2560,2,608]{0,2,1:T(8,128)(2,1)S(1)}, bf16[2560,2,608]{0,2,1:T(8,128)(2,1)}, u32[]{:S(2)}) copy-start(bf16[2560,2,608]{0,2,1:T(8,128)(2,1)} %param.24) | copy-start | bytes 18677764

commit v2 on v1

--- a/solution.py
+++ b/solution.py
@@ -19,40 +19,87 @@
 bf16 = jnp.bfloat16
 
 
-def call(kernel, out_shapes, operands, scratch=(), scalars=0, limit=24):
-    smem = pl.BlockSpec(memory_space=pltpu.SMEM)
-    vmem = pl.BlockSpec(memory_space=pltpu.VMEM)
+def call(kernel, out_shapes, operands, scratch=(), scalars=0, limit=24, in_place=()):
+    spaces = [pltpu.SMEM] * scalars + [pltpu.VMEM] * (len(operands) - scalars)
+    for i in in_place:
+        spaces[i] = pltpu.HBM
+    operands = [
+        pltpu.with_memory_space_constraint(x, pltpu.HBM) if i in in_place else x
+        for i, x in enumerate(operands)
+    ]
     single = isinstance(out_shapes, tuple)
     outs = [out_shapes] if single else out_shapes
     result = pl.pallas_call(
         kernel,
         out_shape=[jax.ShapeDtypeStruct(*o) for o in outs],
-        in_specs=[smem] * scalars + [vmem] * (len(operands) - scalars),
-        out_specs=[vmem] * len(outs),
+        in_specs=[pl.BlockSpec(memory_space=space) for space in spaces],
+        out_specs=[pl.BlockSpec(memory_space=pltpu.VMEM)] * len(outs),
         scratch_shapes=list(scratch),
         compiler_params=pltpu.CompilerParams(vmem_limit_bytes=limit << 20),
     )(*operands)
     return result[0] if single else result
 
 
+def place(index_ref):
+    index = index_ref[0]
+    return index // 16, index // 2 % 8, index % 2
+
+
 def exchange(blocks, axes):
     return lax.all_to_all(blocks, axes, split_axis=0, concat_axis=0, tiled=True)
 
 
-def project_kernel(n_ref, states_ref, gain_ref, w_ref, out_ref, normed_ref):
+def project_kernel(
+    index_ref,
+    states_hbm,
+    gain_hbm,
+    w_hbm,
+    qg_hbm,
+    kg_hbm,
+    out_ref,
+    gains_ref,
+    states_ref,
+    gain_ref,
+    w_ref,
+    normed_ref,
+    sems,
+):
     parts, part_width, head_dim = w_ref.shape
-    x = states_ref[...].astype(f32)
-    inverse = lax.rsqrt(jnp.mean(x * x, axis=-1, keepdims=True) + epsilon)
-    normed_ref[...] = (x * inverse * gain_ref[...]).astype(bf16)
-    start = pl.multiple_of(n_ref[0] * part_width, lane)
-    own = normed_ref[:, pl.ds(start, part_width)]
+    width = states_ref.shape[1]
+    copies = [
+        pltpu.make_async_copy(states_hbm, states_ref, sems.at[0]),
+        pltpu.make_async_copy(gain_hbm, gain_ref, sems.at[1]),
+        pltpu.make_async_copy(qg_hbm, gains_ref.at[0], sems.at[2]),
+        pltpu.make_async_copy(kg_hbm, gains_ref.at[1], sems.at[3]),
+    ]
+    weights = [
+        pltpu.make_async_copy(w_hbm.at[c], w_ref.at[c], sems.at[4 + c]) for c in range(parts)
+    ]
+    for copy in copies + weights:
+        copy.start()
+    copies[0].wait()
+    square = jnp.zeros((states_ref.shape[0], lane), f32)
+    for c in range(width // lane):
+        x = states_ref[:, c * lane : (c + 1) * lane].astype(f32)
+        square = square + x * x
+    inverse = lax.rsqrt(jnp.sum(square, axis=1, keepdims=True) * (1.0 / width) + epsilon)
+    copies[1].wait()
+    for c in range(width // lane):
+        span = slice(c * lane, (c + 1) * lane)
+        x = states_ref[:, span].astype(f32)
+        normed_ref[:, span] = (x * inverse * gain_ref[c : c + 1, :]).astype(bf16)
+    narrow = place(index_ref)[2]
+    own = normed_ref[:, pl.ds(pl.multiple_of(narrow * part_width, lane), part_width)]
     for c in range(parts):
+        weights[c].wait()
         out_ref[:, c * head_dim : (c + 1) * head_dim] = jnp.dot(
             own, w_ref[c], preferred_element_type=f32
         )
-
-
-def query_kernel(own_ref, other_ref, cos_ref, sin_ref, qg_ref, kg_ref, rows_ref, send_ref):
+    copies[2].wait()
+    copies[3].wait()
+
+
+def query_kernel(own_ref, other_ref, cos_ref, sin_ref, gains_ref, first_ref, rows_ref, send_ref):
     head_dim = cos_ref.shape[1]
     copies, _, width = send_ref.shape
     group = width // head_dim
@@ -60,7 +107,7 @@
     cosine, sine = cos_ref[...], sin_ref[...]
     for c in range(group + 1):
         u = proj[:, c * head_dim : (c + 1) * head_dim]
-        gain = qg_ref[...] if c < group else kg_ref[...]
+        gain = gains_ref[0:1, :] if c < group else gains_ref[1:2, :]
         u = u * lax.rsqrt(jnp.mean(u * u, axis=-1, keepdims=True) + epsilon) * gain
         v = (u * cosine + pltpu.roll(u, head_dim // 2, 1) * sine).astype(bf16)
         rows_ref[:, c * head_dim : (c + 1) * head_dim] = v.astype(f32)
@@ -73,12 +120,23 @@
     )
 
 
-def slot_kernel(p_ref, n_ref, pages_ref, len_ref, member_ref, count_ref, owner_ref):
+def slot_kernel(
+    index_ref, pages_hbm, len_hbm, member_ref, count_ref, owner_ref, pages_ref, len_ref, sems
+):
+    copies = [
+        pltpu.make_async_copy(pages_hbm, pages_ref, sems.at[0]),
+        pltpu.make_async_copy(len_hbm, len_ref.at[0], sems.at[1]),
+    ]
+    for copy in copies:
+        copy.start()
+    for copy in copies:
+        copy.wait()
     slot_count, req_count = member_ref.shape
     max_blocks = pages_ref.shape[0]
     half_page = code_span // 2
-    first_slot = (p_ref[0] * slot_count).astype(f32)
-    first_token = (n_ref[0] * half_page).astype(f32)
+    pool, _, narrow = place(index_ref)
+    first_slot = (pool * slot_count).astype(f32)
+    first_token = (narrow * half_page).astype(f32)
     lengths = len_ref[...].astype(f32)
     pages = pages_ref[...].astype(f32)
     request = lax.broadcasted_iota(jnp.int32, (1, req_count), 1).astype(f32)
@@ -113,16 +171,19 @@
 
 def attend_kernel(
     q_ref,
-    k_ref,
-    v_ref,
+    k_hbm,
+    v_hbm,
     member_ref,
     count_ref,
     owner_ref,
     out_ref,
+    k_ref,
+    v_ref,
     qs_ref,
     o_ref,
     ml_ref,
     req_ref,
+    sems,
 ):
     slot_count, half_page, head_dim = k_ref.shape
     req_count = member_ref.shape[1]
@@ -130,16 +191,28 @@
     group = o_ref.shape[0]
     peers = out_ref.shape[0]
     rows = req_count // peers
+    chunks = sems.shape[1]
+    chunk = slot_count // chunks
     scale = head_dim ** (-0.5)
     block = 8
+
+    def copies(i):
+        span = pl.ds(i * chunk, chunk)
+        return (
+            pltpu.make_async_copy(k_hbm.at[span], k_ref.at[span], sems.at[0, i]),
+            pltpu.make_async_copy(v_hbm.at[span], v_ref.at[span], sems.at[1, i]),
+        )
+
+    for i in range(chunks):
+        for copy in copies(i):
+            copy.start()
     queries = q_ref[...].reshape(req_count, group * head_dim)
     qs_ref[...] = jnp.dot(member_ref[...], queries, preferred_element_type=f32)
     columns = block * half_page
     relative = lax.broadcasted_iota(jnp.int32, (block, columns), 1) - (
         half_page * lax.broadcasted_iota(jnp.int32, (block, columns), 0)
     )
-    relative = relative.astype(f32)
-    positive = relative >= 0.0
+    relative = jnp.where(relative >= 0, relative, columns).astype(f32)
     spot = lax.broadcasted_iota(jnp.int32, (block, lane), 1)
     o_ref[:, slot_count:, :] = jnp.zeros((group, padded - slot_count, head_dim), bf16)
     ml_ref[slot_count:, :] = jnp.where(
@@ -147,37 +220,46 @@
     )
 
     def step(i, carry):
-        outs = []
-        for half in range(2):
-            base = pl.multiple_of(i * (2 * block) + half * block, block)
+        k_copy, v_copy = copies(i)
+        k_copy.wait()
+        bases = [pl.multiple_of(i * chunk + b * block, block) for b in range(chunk // block)]
+        scores = []
+        for base in bases:
             qb = qs_ref[pl.ds(base, block), :]
             q = jnp.concatenate(
                 [qb[:, g * head_dim : (g + 1) * head_dim] for g in range(group)], axis=0
             ).astype(bf16)
             k = k_ref[pl.ds(base, block)].reshape(columns, head_dim)
-            v = v_ref[pl.ds(base, block)].reshape(columns, head_dim)
-            s = lax.dot_general(q, k, (((1,), (1,)), ((), ())), preferred_element_type=f32)
+            scores.append(
+                lax.dot_general(q, k, (((1,), (1,)), ((), ())), preferred_element_type=f32)
+            )
+        weights, tops, totals = [], [], []
+        for base, s in zip(bases, scores):
             s = s.reshape(group, block, columns) * scale
-            count = count_ref[pl.ds(base, block), :1]
-            live = (positive & (relative < count))[None]
+            live = (relative < count_ref[pl.ds(base, block), :1])[None]
             s = jnp.where(live, s, masked_score)
             top = jnp.max(s, axis=-1, keepdims=True)
             p = jnp.where(live, jnp.exp(s - top), 0.0)
-            total = jnp.sum(p, axis=-1, keepdims=True)
-            o = jnp.dot(
-                p.reshape(group * block, columns).astype(bf16), v, preferred_element_type=f32
-            )
+            tops.append(top)
+            totals.append(jnp.sum(p, axis=-1, keepdims=True))
+            weights.append(p.reshape(group * block, columns).astype(bf16))
+        v_copy.wait()
+        outs = []
+        for base, p in zip(bases, weights):
+            v = v_ref[pl.ds(base, block)].reshape(columns, head_dim)
+            o = jnp.dot(p, v, preferred_element_type=f32)
             outs.append(o.reshape(group, block, head_dim))
+        for base, top, total in zip(bases, tops, totals):
             stat = jnp.zeros((block, lane), f32)
             for g in range(group):
                 stat = jnp.where(spot == g, top[g], stat)
                 stat = jnp.where(spot == group + g, total[g], stat)
             ml_ref[pl.ds(base, block), :] = stat
-        base = pl.multiple_of(i * (2 * block), 2 * block)
-        o_ref[:, pl.ds(base, 2 * block), :] = jnp.concatenate(outs, axis=1).astype(bf16)
+        first = pl.multiple_of(i * chunk, 2 * block)
+        o_ref[:, pl.ds(first, chunk), :] = jnp.concatenate(outs, axis=1).astype(bf16)
         return carry
 
-    lax.fori_loop(0, slot_count // (2 * block), step, 0, unroll=2)
+    lax.fori_loop(0, chunks, step, 0)
 
     stats = jnp.transpose(ml_ref[...])
     request = lax.broadcasted_iota(jnp.int32, (req_count, 1), 0).astype(f32)
@@ -199,10 +281,9 @@
     req_ref[group] = (
         high + pltpu.roll(middle, 2 * group, 1) + pltpu.roll(low, 4 * group, 1)
     )
-    blank = jnp.zeros((out_ref.shape[1] - (group + 1) * rows, lane), f32)
     for d in range(peers):
         pieces = [req_ref[g, d * rows : (d + 1) * rows, :] for g in range(group + 1)]
-        out_ref[d] = jnp.concatenate(pieces + [blank], axis=0).astype(bf16)
+        out_ref[d] = jnp.concatenate(pieces, axis=0).astype(bf16)
 
 
 def write_units(units_ref, values, out_ref, first, step, parts, units):
@@ -213,14 +294,14 @@
         out_ref[first + step * w] = units_ref[w * units : w * units + unit_pad, :].astype(bf16)
 
 
-def combine_kernel(n_ref, got_ref, rows_ref, w_ref, out_ref, units_ref):
+def combine_kernel(index_ref, got_ref, rows_ref, w_ref, out_ref, units_ref):
     peers = got_ref.shape[0]
     group = w_ref.shape[0] // lane
     rows = rows_ref.shape[0] // 2
     parts = out_ref.shape[0]
     units = rows * w_ref.shape[1] // lane // parts
     scale = lane ** (-0.5)
-    own = rows_ref[pl.ds(pl.multiple_of(n_ref[0] * rows, 8), rows), :]
+    own = rows_ref[pl.ds(pl.multiple_of(place(index_ref)[2] * rows, 8), rows), :]
     key = own[:, group * lane : (group + 1) * lane]
     value = own[:, (group + 1) * lane : (group + 2) * lane]
     spot = lax.broadcasted_iota(jnp.int32, (rows, lane), 1)
@@ -231,7 +312,7 @@
     top = own_score
     stats = []
     for d in range(peers):
-        packed = got_ref[d, group * rows : (group + 2) * rows, :].astype(f32)[:rows]
+        packed = got_ref[d, group * rows :, :].astype(f32)
         stat = (
             packed
             + pltpu.roll(packed, lane - 2 * group, 1)
@@ -258,7 +339,7 @@
     write_units(units_ref, mixed, out_ref, 0, 1, parts, units)
 
 
-def residual_kernel(w_ref, n_ref, got_ref, states_ref, send_ref, resid_ref, units_ref):
+def residual_kernel(index_ref, got_ref, states_ref, send_ref, resid_ref, units_ref):
     parts = got_ref.shape[0]
     rows = states_ref.shape[0] // 2
     width = states_ref.shape[1]
@@ -269,13 +350,14 @@
     for d in range(send_ref.shape[0]):
         send_ref[d] = mixed.astype(bf16)
     states = states_ref[...].astype(f32)
-    states = jnp.where(n_ref[0] == 0, states[:rows], states[rows:])
+    _, wide, narrow = place(index_ref)
+    states = jnp.where(narrow == 0, states[:rows], states[rows:])
     for c in range(width // lane):
         units_ref[c * rows : (c + 1) * rows, :] = states[:, c * lane : (c + 1) * lane]
     units_ref[rows * width // lane :, :] = jnp.zeros((8, lane), f32)
     for w in range(parts):
 
-        @pl.when(w_ref[0] == w)
+        @pl.when(wide == w)
         def _():
             resid_ref[...] = mixed + units_ref[w * units : w * units + unit_pad, :]
 
@@ -287,12 +369,25 @@
 
 
 def hidden_kernel(
-    got_ref, states_ref, gain_ref, wg_ref, wd_ref, mixed_ref, out_ref, units_ref, x_ref, flat_ref
+    got_ref,
+    states_ref,
+    gain_hbm,
+    wg_ref,
+    wd_ref,
+    mixed_ref,
+    out_ref,
+    units_ref,
+    x_ref,
+    flat_ref,
+    gain_ref,
+    sem,
 ):
     rows, width = states_ref.shape
     half = rows // 2
     parts = got_ref.shape[0] // 2
     units = half * width // lane // parts
+    gain_copy = pltpu.make_async_copy(gain_hbm, gain_ref, sem)
+    gain_copy.start()
     read_units(got_ref, units_ref, parts, units)
     square = jnp.zeros((rows, lane), f32)
     for c in range(width // lane):
@@ -305,7 +400,14 @@
         x_ref[:, span] = resid
         square = square + resid * resid
     inverse = lax.rsqrt(jnp.sum(square, axis=1, keepdims=True) * (1.0 / width) + epsilon)
-    normed = (x_ref[...] * inverse * gain_ref[...]).astype(bf16)
+    gain_copy.wait()
+    normed = jnp.concatenate(
+        [
+            (x_ref[:, c * lane : (c + 1) * lane] * inverse * gain_ref[c : c + 1, :]).astype(bf16)
+            for c in range(width // lane)
+        ],
+        axis=1,
+    )
     contract = (((1,), (1,)), ((), ()))
     gate = lax.dot_general(normed, wg_ref[0], contract, preferred_element_type=f32)
     up = lax.dot_general(normed, wg_ref[1], contract, preferred_element_type=f32)
@@ -361,9 +463,7 @@
     holders = lax.axis_size("pool")
     peers = holders * narrow_size
     split = wide_size * narrow_size
-    narrow = lax.axis_index("narrow").reshape(1)
-    wide = lax.axis_index("wide").reshape(1)
-    pool = lax.axis_index("pool").reshape(1)
+    index = lax.axis_index(("pool", "wide", "narrow")).reshape(1)
     rows, width = states.shape
     half = rows // narrow_size
     req_count = page_table.shape[0]
@@ -374,16 +474,23 @@
     slot_pad = -(-slot_count // lane) * lane
     half_units = half * width // lane
 
-    partial_proj = call(
+    partial_proj, gains = call(
         project_kernel,
-        ((rows, parts * head_dim), f32),
-        [narrow, states, gain_in[None], w_qkv[:, 0].swapaxes(0, 1)],
-        [pltpu.VMEM((rows, width), bf16)],
+        [((rows, parts * head_dim), f32), ((2, head_dim), f32)],
+        [index, states, gain_in.reshape(-1, lane), w_qkv[:, 0].swapaxes(0, 1), q_gain, k_gain],
+        [
+            pltpu.VMEM((rows, width), bf16),
+            pltpu.VMEM((width // lane, lane), f32),
+            pltpu.VMEM((parts, w_qkv.shape[0], head_dim), bf16),
+            pltpu.VMEM((rows, width), bf16),
+            pltpu.SemaphoreType.DMA((4 + parts,)),
+        ],
         scalars=1,
+        in_place=(1, 2, 3, 4, 5),
     )
     swap = [(i, narrow_size - 1 - i) for i in range(narrow_size)]
     other_proj = lax.ppermute(partial_proj, "narrow", swap)
-    own_len = lax.dynamic_slice_in_dim(cache_len, pool[0] * rows, rows, 0).astype(f32)
+    own_len = lax.dynamic_slice_in_dim(cache_len, lax.axis_index("pool") * rows, rows, 0).astype(f32)
     ramp = jnp.arange(head_dim // 2).astype(f32)
     freqs = jnp.exp(ramp * (-2.0 * math.log(rope_base) / head_dim))
     angle = own_len[:, None] * freqs
@@ -397,31 +504,42 @@
             ((slot_count, lane), f32),
             ((8, slot_pad), f32),
         ],
-        [pool, narrow, page_table.T, cache_len[None]],
-        scalars=2,
+        [index, page_table.T, cache_len],
+        [
+            pltpu.VMEM((page_table.shape[1], req_count), jnp.int32),
+            pltpu.VMEM((1, req_count), jnp.int32),
+            pltpu.SemaphoreType.DMA((2,)),
+        ],
+        scalars=1,
+        in_place=(1, 2),
     )
     qkv_rows, sent = call(
         query_kernel,
         [((rows, parts * head_dim), f32), ((holders, rows, group * head_dim), bf16)],
-        [partial_proj, other_proj, cosine, sine, q_gain[None], k_gain[None]],
+        [partial_proj, other_proj, cosine, sine, gains, owner],
     )
     queries = exchange(sent, "pool")
     payload = call(
         attend_kernel,
-        ((peers, lane, lane), bf16),
+        ((peers, (group + 1) * half, lane), bf16),
         [queries, keys, values, member, count, owner],
         [
+            pltpu.VMEM(keys.shape, bf16),
+            pltpu.VMEM(values.shape, bf16),
             pltpu.VMEM((slot_count, group * head_dim), f32),
             pltpu.VMEM((group, slot_pad, head_dim), bf16),
             pltpu.VMEM((slot_pad, lane), f32),
             pltpu.VMEM((group + 1, req_count, head_dim), f32),
+            pltpu.SemaphoreType.DMA((2, 3)),
         ],
+        in_place=(1, 2),
+        limit=32,
     )
     got = exchange(payload, ("pool", "narrow"))
     sent = call(
         combine_kernel,
         ((wide_size, unit_pad, lane), bf16),
-        [narrow, got, qkv_rows, w_out],
+        [index, got, qkv_rows, w_out],
         [pltpu.VMEM((half_units + 8, lane), f32)],
         scalars=1,
     )
@@ -429,21 +547,24 @@
     sent, resid_units = call(
         residual_kernel,
         [((split, unit_pad, lane), bf16), ((unit_pad, lane), f32)],
-        [wide, narrow, got, states],
+        [index, got, states],
         [pltpu.VMEM((half_units + 8, lane), f32)],
-        scalars=2,
+        scalars=1,
     )
     both = ("wide", "narrow")
     got = exchange(sent, both)
     attn_mixed, sent = call(
         hidden_kernel,
         [((rows, width), bf16), ((split, unit_pad, lane), bf16)],
-        [got, states, gain_post[None], w_gate_up.transpose(1, 2, 0), w_down],
+        [got, states, gain_post.reshape(-1, lane), w_gate_up.transpose(1, 2, 0), w_down],
         [
             pltpu.VMEM((narrow_size, half_units, lane), f32),
             pltpu.VMEM((rows, width), f32),
             pltpu.VMEM((half_units + 8, lane), f32),
+            pltpu.VMEM((width // lane, lane), f32),
+            pltpu.SemaphoreType.DMA(()),
         ],
+        in_place=(2,),
     )
     got = exchange(sent, both)
     sent = call(total_kernel, ((split, unit_pad, lane), bf16), [got, resid_units])

time: 119 us -> 99.3 us (0.83)
  blocking collectives: 38.9 us -> 78 us
  waiting for transfers between devices: 26 us -> 1.28 us
  starting transfers between devices: 18.1 us -> 2.09 us
  local copies, waits for them, and re-layouts: 14.9 us -> 0.02 us
  Pallas kernels: 19 us -> 15.8 us
    all_to_all x3 -> x6, blocking collectives: 38.9 us -> 78 us  [exchange(): return lax.all_to_all(blocks, axes, split_axis=0, concat_axis=0, tiled=True)]
    all_to_all x3 -> x0, waiting for transfers between devices: 23.1 us -> none  [exchange(): return lax.all_to_all(blocks, axes, split_axis=0, concat_axis=0, tiled=True)]
    all_to_all x3 -> x0, starting transfers between devices: 16 us -> none  [exchange(): return lax.all_to_all(blocks, axes, split_axis=0, concat_axis=0, tiled=True)]
    unnamed x28 -> x10, local copies, waits for them, and re-layouts: 13.5 us -> 0.02 us
    pallas_call x9, Pallas kernels: 19 us -> 15.8 us  [call(): pl.pallas_call(kernel, out_shape=[jax.ShapeDtypeStruct(*o) for o in outs]...]
    ppermute x1, waiting for transfers between devices: 2.83 us -> 1.28 us  [per_device(): other_proj = lax.ppermute(partial_proj, 'narrow', swap)]
    broadcast_in_dim x3 -> x0, local copies, waits for them, and re-layouts: 1.41 us -> none  [the longest x1 0.72 us: per_device(): gain_in[None]]
  transfers between devices with their start and end apart: 4 -> 1, of which waited for: 4 -> 1; matrix products, arithmetic and copies ran while one was open for 1% -> 1% of each run, Pallas kernels for 1% -> 2%
where the time goes in v2:
time: 99.3 us; the launch traced here: 98.9 us
  blocking collectives  78 us (79%)
  Pallas kernels  15.8 us (16%)
  starting transfers between devices  2.09 us (2%)
  waiting for transfers between devices  1.28 us (1%)
  other arithmetic  1.02 us (1%)
    all_to_all x6, blocking collectives, exchange(): return lax.all_to_all(blocks, axes, split_axis=0, concat_axis=0, tiled=True)  78 us
    pallas_call x9, Pallas kernels, call(): pl.pallas_call(kernel, out_shape=[jax.ShapeDtypeStruct(*o) for o in outs]...  15.8 us
    ppermute x1, starting transfers between devices, per_device(): other_proj = lax.ppermute(partial_proj, 'narrow', swap)  2.09 us
  transfers between devices with their start and end apart: 1, of which 1 were waited for; matrix products, arithmetic and copies ran while one was open for 1% of the time, Pallas kernels for 2%

profile of v2, /device:TPU:0, one launch (start us, length us, event | category | flops | bytes accessed | tf_op | source)
XLA Modules:
  0.0 98.9 jit_solution(13444107353955503055)
XLA Ops:
  0.6 2.4 %shard_map.140 = (f32[48,768]{1,0:T(8,128)S(1)}, f32[2,128]{1,0:T(2,128)S(1)}) custom-call(s32[1]{0:T(128)} %bitcast.index_ref, bf16[48,2560]{1,0:T(8,128)(2,1)} %states_ref.3, f32[20,128]{1,0:T(8,128)} %bitcast.17, bf16[6,1280,128]{2,1,0:T(8,128)(2,1)} %bitcast.15, f32[128]{0:T(128)} %qg_hbm.1, f32[128]{0:T(128)} %kg_hbm.1), custom_call_target="tpu_custom_call" | custom-call | tf_op jit(solution)/shard_map/pallas_call | solution.py:32
  3.1 2.1 %collective-permute-start = (f32[48,768]{1,0:T(8,128)S(1)}, f32[48,768]{1,0:T(8,128)S(1)}, u32[]{:S(2)}, u32[]{:S(2)}) collective-permute-start(f32[48,768]{1,0:T(8,128)S(1)} %get-tuple-element.13.own_ref), channel_id=1, source_target_pairs={{0,1},{1,0},{2,3},{3,2},{4,5},{5,4},{6,7},{7,6},{8,9},{9,8},{10,11... | collective-permute-start | bytes 442376 | tf_op jit(solution)/shard_map/ppermute | solution.py:492
  5.2 0.8 dynamic-slice_convert_fusion
  5.9 0.2 fusion
  6.1 1.5 %shard_map.141 = (bf16[288,384]{1,0:T(8,128)(2,1)S(1)}, f32[288,128]{1,0:T(8,128)S(1)}, f32[8,384]{1,0:T(8,128)S(1)}) custom-call(s32[1]{0:T(128)} %bitcast.index_ref, s32[64,384]{1,0:T(8,128)} %bitcast.16, s32[384]{0:T(512)} %len_hbm.1), custom_call_target="tpu_custom_call" | custom-call | tf_op jit(solution)/shard_map/pallas_call | solution.py:32
  7.6 0.1 pad_maximum_fusion
  7.7 1.3 %collective-permute-done.other_ref = f32[48,768]{1,0:T(8,128)S(1)} collective-permute-done((f32[48,768]{1,0:T(8,128)S(1)}, f32[48,768]{1,0:T(8,128)S(1)}, u32[]{:S(2)}, u32[]{:S(2)}) %collective-permute-start) | collective-permute-done | bytes 147488 | tf_op jit(solution)/shard_map/ppermute | solution.py:492
  9.0 0.2 shard_map.142
  9.2 13.0 %all_to_all.30.q_ref = bf16[8,48,512]{2,1,0:T(8,128)(2,1)S(1)} all-to-all(bf16[8,48,512]{2,1,0:T(8,128)(2,1)S(1)} %get-tuple-element.16), channel_id=1, replica_groups=mesh['pool'=8,'wide'=8,'narrow'=2] {'pool'}, dimensions={0} | all-to-all | bytes 786432 | tf_op jit(solution)/shard_map/all_to_all | solution.py:49
  22.3 0.0 slice-start
  22.3 0.0 copy-start.1
  22.3 0.0 slice-start.1
  22.3 6.4 %shard_map.143 = bf16[16,120,128]{2,1,0:T(8,128)(2,1)S(1)} custom-call(bf16[8,48,512]{2,1,0:T(8,128)(2,1)S(1)} %all_to_all.30.q_ref, bf16[288,64,128]{2,1,0:T(8,128)(2,1)} %bitcast.13, bf16[288,64,128]{2,1,0:T(8,128)(2,1)} %bitcast.14, bf16[288,384]{1,0:T(8,128)(2,1)S(1)} %get-tuple-element.17.member_ref, f32[288,128]{1,0:T(8,128)S(1)} %get-tuple-element.18.count_ref, ...), custom_call_target="tpu_custom_call" | custom-call | tf_op jit(solution)/shard_map/pallas_call | solution.py:32
  28.7 0.0 copy-start.2
  28.7 0.0 copy-start
  28.8 14.6 %all_to_all.31.got_ref = bf16[16,120,128]{2,1,0:T(8,128)(2,1)S(1)} all-to-all(bf16[16,120,128]{2,1,0:T(8,128)(2,1)S(1)} %shard_map.143), channel_id=1, replica_groups=mesh['pool'=8,'wide'=8,'narrow'=2] {'pool','narrow'}, dimensions={0} | all-to-all | bytes 983040 | tf_op jit(solution)/shard_map/all_to_all | solution.py:49
  43.4 0.0 copy-done.1
  43.4 1.0 %shard_map.144 = bf16[8,64,128]{2,1,0:T(8,128)(2,1)S(1)} custom-call(s32[1]{0:T(128)} %bitcast.index_ref, bf16[16,120,128]{2,1,0:T(8,128)(2,1)S(1)} %all_to_all.31.got_ref, f32[48,768]{1,0:T(8,128)S(1)} %get-tuple-element.19.rows_ref, bf16[512,2560]{1,0:T(8,128)(2,1)S(1)} %copy-done.1), custom_call_target="tpu_custom_call" | custom-call | tf_op jit(solution)/shard_map/pallas_call | solution.py:32
  44.4 15.2 %all_to_all.32.got_ref = bf16[8,64,128]{2,1,0:T(8,128)(2,1)S(1)} all-to-all(bf16[8,64,128]{2,1,0:T(8,128)(2,1)S(1)} %shard_map.144), channel_id=1, replica_groups=mesh['pool'=8,'wide'=8,'narrow'=2] {'wide'}, dimensions={0} | all-to-all | bytes 262144 | tf_op jit(solution)/shard_map/all_to_all | solution.py:49
  59.6 0.0 copy-done.2
  59.6 0.1 shard_map.145
  59.7 11.3 %all_to_all.33.got_ref = bf16[16,64,128]{2,1,0:T(8,128)(2,1)S(1)} all-to-all(bf16[16,64,128]{2,1,0:T(8,128)(2,1)S(1)} %get-tuple-element.20), channel_id=1, replica_groups=mesh['pool'=8,'wide'=8,'narrow'=2] {'wide','narrow'}, dimensions={0} | all-to-all | bytes 524288 | tf_op jit(solution)/shard_map/all_to_all | solution.py:49
  71.0 0.0 slice-done
  71.0 0.0 slice-done.1
  71.0 0.0 copy-done
  71.0 3.2 %shard_map.146 = (bf16[48,2560]{1,0:T(8,128)(2,1)}, bf16[16,64,128]{2,1,0:T(8,128)(2,1)S(1)}) custom-call(bf16[16,64,128]{2,1,0:T(8,128)(2,1)S(1)} %all_to_all.33.got_ref, bf16[48,2560]{1,0:T(8,128)(2,1)S(1)} %copy-done.2, f32[20,128]{1,0:T(8,128)} %bitcast.18, bf16[2,608,2560]{2,1,0:T(8,128)(2,1)S(1)} %bitcast.12, bf16[608,2560]{1,0:T(8,128)(2,1)S(1)} %copy-done), custom_call_target="tpu_custom_call" | custom-call | tf_op jit(solution)/shard_map/pallas_call | solution.py:32
  74.2 11.9 %all_to_all.34.got_ref = bf16[16,64,128]{2,1,0:T(8,128)(2,1)S(1)} all-to-all(bf16[16,64,128]{2,1,0:T(8,128)(2,1)S(1)} %get-tuple-element.22), channel_id=1, replica_groups=mesh['pool'=8,'wide'=8,'narrow'=2] {'wide','narrow'}, dimensions={0} | all-to-all | bytes 524288 | tf_op jit(solution)/shard_map/all_to_all | solution.py:49
  86.2 11.9 %all_to_all.35.got_ref = bf16[16,64,128]{2,1,0:T(8,128)(2,1)S(1)} all-to-all(bf16[16,64,128]{2,1,0:T(8,128)(2,1)S(1)} %shard_map.147), channel_id=1, replica_groups=mesh['pool'=8,'wide'=8,'narrow'=2] {'wide','narrow'}, dimensions={0} | all-to-all | bytes 524288 | tf_op jit(solution)/shard_map/all_to_all | solution.py:49
  98.2 0.7 shard_map.148
  (3 shorter events, 0.1 us)
Async XLA Ops:
  3.1 5.9 %collective-permute-start = (f32[48,768]{1,0:T(8,128)S(1)}, f32[48,768]{1,0:T(8,128)S(1)}, u32[]{:S(2)}, u32[]{:S(2)}) collective-permute-start(f32[48,768]{1,0:T(8,128)S(1)} %get-tuple-element.13.own_ref), channel_id=1, source_target_pairs={{0,1},{1,0},{2,3},{3,2},{4,5},{5,4},{6,7},{7,6},{8,9},{9,8},{10,11... | collective-permute-start | bytes 442376 | tf_op jit(solution)/shard_map/ppermute | solution.py:492
  22.3 48.7 %slice-start = ((s8[6225920]{0:T(1024)(128)(4,1)}), s8[4194304]{0:T(1024)(128)(4,1)S(1)}, s32[]{:S(2)}) async-start(s8[6225920]{0:T(1024)(128)(4,1)} %bitcast.10), calls=%async_computation.6 | async-start | bytes 8388608
  22.3 21.1 %copy-start.1 = (bf16[512,2560]{1,0:T(8,128)(2,1)S(1)}, bf16[512,2560]{1,0:T(8,128)(2,1)}, u32[]{:S(2)}) copy-start(bf16[512,2560]{1,0:T(8,128)(2,1)} %w_ref.1) | copy-start | bytes 7864324
  22.3 48.7 %slice-start.1 = ((s8[6225920]{0:T(1024)(128)(4,1)}), s8[2031616]{0:T(1024)(128)(4,1)S(1)}, s32[]{:S(2)}) async-start(s8[6225920]{0:T(1024)(128)(4,1)} %bitcast.10), calls=%async_computation.7 | async-start | bytes 4063232
  28.7 30.9 %copy-start.2 = (bf16[48,2560]{1,0:T(8,128)(2,1)S(1)}, bf16[48,2560]{1,0:T(8,128)(2,1)}, u32[]{:S(2)}) copy-start(bf16[48,2560]{1,0:T(8,128)(2,1)} %states_ref.3) | copy-start | bytes 737284
  28.7 42.2 %copy-start = (bf16[608,2560]{1,0:T(8,128)(2,1)S(1)}, bf16[608,2560]{1,0:T(8,128)(2,1)}, u32[]{:S(2)}) copy-start(bf16[608,2560]{1,0:T(8,128)(2,1)} %wd_ref.1) | copy-start | bytes 9338884
